TPU v7x, 32 devices: a whole 2x2x4 slice. The times are simulated.
32 devices in a mesh: grp: 2 (over y), ft: 4 (over z), bl: 4 (over x, core).
Axes of the slice: x: 2, y: 2, z: 4, core: 2. Of those that a mesh axis runs over, the one named last changes fastest.
Arguments:
- voltages: bfloat16 [2, 16384, 1024], P(None, ('grp', 'ft'), 'bl'), parts along dimension 1, may hold values from -11 to 11
- coefs: float32 [8, 2048], replicated, may hold values from -2 to 2
- block_ids: int32 [4], replicated, may hold values from 0 to 3, each once
- tile_owner: int32 [20], P('grp'), parts along dimension 0, may hold values from 0 to 3, as said below
Outputs:
- vis: float32 [2, 64, 20, 256, 256], P(None, ('grp', 'ft'), 'bl'), parts along dimension 1
There are 2 independent parts, one for each index of `grp`. A program takes and returns all parts, laid end to end along the dimension named above; an argument that names none is the same for every part. Nothing has to cross between parts.
Inputs may be any that keep to these rules, and one draw needn't show every extreme that they name: tile_owner[t] is the index along bl of the device that owns tile t; one owner holds exactly 5 tiles, the others share the remaining tiles as evenly as counts allow.
All inputs are finite; a program needn't handle non-finite values.
Results may differ from a plain program's by a relative error of at most 0.00099.
Values may be sent and summed in bfloat16 or wider, within the bound.
A program may use at most 128 MiB of HBM per device.

v0:
```python
import functools
import math

import jax
import jax.numpy as jnp
import numpy as np
from jax import lax
from jax.experimental import pallas as pl
from jax.experimental.pallas import tpu as pltpu
from jax.sharding import PartitionSpec as P

AVG = 64


def tile_product(row_part, col_part, norm_scale):
    products = jnp.einsum(
        "pscax,qscay->cpqxy", row_part, col_part, preferred_element_type=jnp.float32
    )
    real_part = products[:, 0, 0] + products[:, 1, 1]
    imag_part = products[:, 1, 0] - products[:, 0, 1]
    return jnp.stack([real_part, imag_part]) * norm_scale


def dft_tables(order_len):
    steps_one = jnp.arange(order_len, dtype=jnp.int32)
    phase_grid = steps_one[:, None] * steps_one[None, :] % order_len
    angles = phase_grid.astype(jnp.float32) * (2.0 * math.pi / order_len)
    return (jnp.cos(angles), jnp.sin(angles))


def transform(filtered):
    per_dev = filtered.shape[1]
    chan_count = filtered.shape[2]
    rows_here = filtered.shape[3]
    outer_len = math.isqrt(chan_count)
    while chan_count % outer_len != 0:
        outer_len = outer_len - 1
    inner_len = chan_count // outer_len
    highest = lax.Precision.HIGHEST
    reshaped = filtered.reshape(2, per_dev, outer_len, inner_len, rows_here)
    real_in = reshaped[0]
    imag_in = reshaped[1]
    cos_outer, sin_outer = dft_tables(outer_len)
    section_re = jnp.einsum("snkb,nm->smkb", real_in, cos_outer, precision=highest) + jnp.einsum(
        "snkb,nm->smkb", imag_in, sin_outer, precision=highest
    )
    section_im = jnp.einsum("snkb,nm->smkb", imag_in, cos_outer, precision=highest) - jnp.einsum(
        "snkb,nm->smkb", real_in, sin_outer, precision=highest
    )
    twiddle_grid = (
        jnp.arange(outer_len, dtype=jnp.int32)[:, None]
        * jnp.arange(inner_len, dtype=jnp.int32)[None, :]
        % chan_count
    )
    twiddle_angles = twiddle_grid.astype(jnp.float32) * (2.0 * math.pi / chan_count)
    cos_twiddle = jnp.cos(twiddle_angles)[None, :, :, None]
    sin_twiddle = jnp.sin(twiddle_angles)[None, :, :, None]
    rot_re = section_re * cos_twiddle + section_im * sin_twiddle
    rot_im = section_im * cos_twiddle - section_re * sin_twiddle
    cos_inner, sin_inner = dft_tables(inner_len)
    final_re = jnp.einsum("smkb,kq->sqmb", rot_re, cos_inner, precision=highest) + jnp.einsum(
        "smkb,kq->sqmb", rot_im, sin_inner, precision=highest
    )
    final_im = jnp.einsum("smkb,kq->sqmb", rot_im, cos_inner, precision=highest) - jnp.einsum(
        "smkb,kq->sqmb", rot_re, sin_inner, precision=highest
    )
    stacked = jnp.stack([final_re, final_im]).reshape(2, per_dev, chan_count, rows_here)
    return (stacked * (1.0 / math.sqrt(chan_count))).astype(jnp.bfloat16)


def apply_taps(window, coef_part, taps_count, out_len):
    filtered = jnp.zeros((2, out_len, window.shape[2], window.shape[3]), jnp.float32)
    for tap_index in range(taps_count):
        filtered = filtered + coef_part[tap_index][None, None, :, None] * window[
            :, tap_index : tap_index + out_len
        ].astype(jnp.float32)
    return filtered


def per_device_general(voltages, coefs, block_ids, tile_owner):
    taps_count = coefs.shape[0]
    chan_count = coefs.shape[1]
    rows_here = voltages.shape[2]
    per_dev = voltages.shape[1] // chan_count
    volt_blocks = voltages.reshape(2, per_dev, chan_count, rows_here)
    phase_block = lax.all_to_all(volt_blocks, "ft", split_axis=2, concat_axis=1, tiled=True)
    spectra_count = phase_block.shape[1]
    phase_here = phase_block.shape[2]
    coef_part = lax.dynamic_slice_in_dim(coefs, lax.axis_index("ft") * phase_here, phase_here, 1)
    zero_front = jnp.zeros((2, taps_count - 1, phase_here, rows_here), phase_block.dtype)
    long_window = jnp.concatenate([zero_front, phase_block], axis=1)
    phase_filtered = apply_taps(long_window, coef_part, taps_count, spectra_count)
    filtered = lax.all_to_all(phase_filtered, "ft", split_axis=1, concat_axis=2, tiled=True)
    spectra = transform(filtered)
    turned = lax.all_to_all(spectra, "ft", split_axis=2, concat_axis=1, tiled=True)
    spectra_all = turned.shape[1]
    chan_here = turned.shape[2]
    coarse_here = chan_here // AVG
    coarse_view = turned.reshape(2, spectra_all, coarse_here, AVG, rows_here)
    norm_scale = 1.0 / (AVG * spectra_all)
    block_count = lax.axis_size("bl")
    my_index = lax.axis_index("bl")
    tile_count = block_count * (block_count + 1) // 2
    slot_cap = 2 * tile_count // block_count
    row_table = jnp.asarray(
        np.array(
            [
                first_id
                for first_id in range(block_count)
                for second_id in range(first_id, block_count)
            ],
            dtype=np.int32,
        )
    )
    col_table = jnp.asarray(
        np.array(
            [
                second_id
                for first_id in range(block_count)
                for second_id in range(first_id, block_count)
            ],
            dtype=np.int32,
        )
    )
    tile_pos = jnp.arange(tile_count, dtype=jnp.int32)
    same_owner = tile_owner[None, :] == tile_owner[:, None]
    before_mask = tile_pos[None, :] < tile_pos[:, None]
    slot_rank = jnp.sum((same_owner & before_mask).astype(jnp.int32), axis=1)
    labels = jnp.arange(block_count, dtype=jnp.int32)
    shard_of = jnp.sum(jnp.where(block_ids[None, :] == labels[:, None], labels[None, :], 0), axis=1)
    gathered = lax.all_gather(coarse_view[None], "bl", axis=0, tiled=True)
    mine_mask = tile_owner == my_index
    own_count = jnp.sum(mine_mask.astype(jnp.int32))
    slot_steps = jnp.arange(slot_cap, dtype=jnp.int32)
    slot_tile = jnp.sum(
        jnp.where(
            mine_mask[None, :] & (slot_rank[None, :] == slot_steps[:, None]), tile_pos[None, :], 0
        ),
        axis=1,
    )

    def one_tile(slot_pos, result_tiles):
        tile_id = slot_tile[slot_pos]
        row_block = gathered[shard_of[row_table[tile_id]]]
        col_block = gathered[shard_of[col_table[tile_id]]]
        tile = tile_product(row_block, col_block, norm_scale)
        return lax.dynamic_update_slice(result_tiles, tile[:, :, None], (0, 0, slot_pos, 0, 0))

    empty_tiles = jnp.zeros((2, coarse_here, slot_cap, rows_here, rows_here), jnp.float32)
    return lax.fori_loop(0, own_count, one_tile, empty_tiles)


LANES = 128
RADIX = 16


def split_halves(values):
    high = values.astype(jnp.bfloat16)
    low = (values - high.astype(jnp.float32)).astype(jnp.bfloat16)
    return high, low


def dft_constants(chan_count):
    rows = chan_count // RADIX
    m_grid = np.arange(rows, dtype=np.int64)[None, :, None]
    n_grid = RADIX * np.arange(rows, dtype=np.int64)[None, None, :] + np.arange(RADIX)[:, None, None]
    angles = (m_grid * n_grid % chan_count) * (2.0 * np.pi / chan_count)
    scale = 1.0 / math.sqrt(chan_count)
    parts = []
    for table in (np.cos(angles) * scale, np.sin(angles) * scale):
        high = table.astype(jnp.bfloat16)
        parts.append(high)
        parts.append((table - high.astype(np.float64)).astype(jnp.bfloat16))
    return np.stack([parts[0], parts[2], parts[1], parts[3]], axis=1)


def turn_values(value, step, count):
    re, im = value
    step = step % count
    if step == 0:
        return value
    if 4 * step == count:
        return im, -re
    if 2 * step == count:
        return -re, -im
    if 8 * step == count:
        half = np.float32(math.sqrt(0.5))
        return (re + im) * half, (im - re) * half
    if 8 * step == 3 * count:
        half = np.float32(math.sqrt(0.5))
        return (im - re) * half, -(re + im) * half
    angle = 2.0 * math.pi * step / count
    cos_v, sin_v = np.float32(math.cos(angle)), np.float32(math.sin(angle))
    return re * cos_v + im * sin_v, im * cos_v - re * sin_v


def small_fft(values):
    count = len(values)
    if count == 1:
        return values
    even = small_fft(values[0::2])
    odd = small_fft(values[1::2])
    first, second = [], []
    for pos in range(count // 2):
        turned = turn_values(odd[pos], pos, count)
        first.append((even[pos][0] + turned[0], even[pos][1] + turned[1]))
        second.append((even[pos][0] - turned[0], even[pos][1] - turned[1]))
    return first + second


HALVES = 2
SUBROWS = RADIX // HALVES


def pick_half(values, part):
    rows, lanes = values.shape
    return values.reshape(rows // RADIX, HALVES, SUBROWS, lanes)[:, part].reshape(-1, lanes)


def pack_half(part, volt_ref, first_send):
    half = LANES // 2
    block = 256

    def step(pos, carry):
        rows = pl.ds(pl.multiple_of(pos * block, block), block)
        out_rows = pl.ds(pl.multiple_of(pos * (block // HALVES), block // HALVES), block // HALVES)
        for dest in range(first_send.shape[1]):
            lanes = slice(dest * half, (dest + 1) * half)
            real = pick_half(volt_ref[0, rows, lanes].astype(jnp.float32), part)
            imag = pick_half(volt_ref[1, rows, lanes].astype(jnp.float32), part)
            first_send[part, dest, out_rows, :] = jnp.concatenate([real, imag], axis=1).astype(
                first_send.dtype
            )
        return carry

    lax.fori_loop(0, volt_ref.shape[1] // block, step, 0)


def far_first(me, parts, rank):
    down = parts - 1 - rank
    down = down - (me >= down).astype(jnp.int32)
    up = rank + (me <= rank).astype(jnp.int32)
    return jnp.where(me < parts // 2, down, up)


def turn_coefs(coef_ref, rows_ref):
    block = 256

    def step(pos, carry):
        lanes = pl.ds(pl.multiple_of(pos * block, block), block)
        out_rows = pl.ds(pl.multiple_of(pos * (block // HALVES), block // HALVES), block // HALVES)
        turned = jnp.transpose(coef_ref[:, lanes])
        for part in range(HALVES):
            rows_ref[part, out_rows, :] = pick_half(turned, part)
        return carry

    lax.fori_loop(0, coef_ref.shape[1] // block, step, 0)


def filter_dft(pair, part, data_ref, rows_ref, table_ref, filt_ref, mid_ref):
    taps_count = rows_ref.shape[2]
    rows_half = data_ref.shape[2]
    sub = rows_half // SUBROWS
    half = LANES // 2
    block = 128

    def filter_step(step, carry):
        rows = pl.ds(pl.multiple_of(step * block, block), block)
        coef = rows_ref[part, rows, :]
        low_lane = lax.broadcasted_iota(jnp.int32, (block, LANES), 1) < half
        samples = {}
        for time_pos in range(max(0, 2 * pair - taps_count + 1), 2 * pair + 2):
            samples[time_pos] = data_ref[part, time_pos, rows, :].astype(jnp.float32)
        sums = []
        for spectrum in (2 * pair, 2 * pair + 1):
            total = None
            for tap in range(taps_count):
                time_pos = spectrum - (taps_count - 1) + tap
                if time_pos < 0:
                    continue
                term = coef[:, tap : tap + 1] * samples[time_pos]
                total = term if total is None else total + term
            sums.append(total)
        filt_ref[0, rows, :] = jnp.where(low_lane, sums[0], pltpu.roll(sums[1], half, 1))
        filt_ref[1, rows, :] = jnp.where(low_lane, pltpu.roll(sums[0], half, 1), sums[1])
        return carry

    lax.fori_loop(0, rows_half // block, filter_step, 0)

    def dft_step(offset, carry):
        phase = part * SUBROWS + offset
        real_in = filt_ref[0, pl.ds(offset, sub, stride=SUBROWS), :]
        imag_in = filt_ref[1, pl.ds(offset, sub, stride=SUBROWS), :]
        high, low = split_halves(jnp.concatenate([real_in, imag_in], axis=0))

        def matrix(first):
            cos_m = table_ref[phase, first]
            sin_m = table_ref[phase, first + 1]
            return jnp.concatenate(
                [
                    jnp.concatenate([cos_m, sin_m], axis=1),
                    jnp.concatenate([-sin_m, cos_m], axis=1),
                ],
                axis=0,
            )

        big, small = matrix(0), matrix(2)
        total = jnp.dot(big, low, preferred_element_type=jnp.float32)
        total = total + jnp.dot(small, high, preferred_element_type=jnp.float32)
        total = total + jnp.dot(big, high, preferred_element_type=jnp.float32)
        mid_ref[pair, phase] = total
        return carry

    lax.fori_loop(0, SUBROWS, dft_step, 0, unroll=4)


def radix_pass(pair, mid_ref, send_ref):
    rounds, parts = send_ref.shape[1:3]
    rows_round = send_ref.shape[4]
    sub = mid_ref.shape[2] // 2
    splits = sub // rows_round
    groups = rounds // splits
    rows_step = 16

    for split in range(splits):

        def radix_step(step, carry):
            out_rows = pl.ds(pl.multiple_of(step * rows_step, rows_step), rows_step)
            start = pl.multiple_of(split * rows_round + step * rows_step, rows_step)
            values = [
                (
                    mid_ref[pair, phase, pl.ds(start, rows_step), :],
                    mid_ref[pair, phase, pl.ds(sub + start, rows_step), :],
                )
                for phase in range(RADIX)
            ]
            for group, (re, im) in enumerate(small_fft(values)):
                dest, turn = group // groups, group % groups * splits + split
                send_ref[pair, turn, dest, 0, out_rows, :] = re.astype(jnp.bfloat16)
                send_ref[pair, turn, dest, 1, out_rows, :] = im.astype(jnp.bfloat16)
            return carry

        lax.fori_loop(0, rows_round // rows_step, radix_step, 0)


def merge_round(pair, turn, recv_ref, own_ref):
    half = LANES // 2
    sources = recv_ref.shape[2]
    coarse_round = recv_ref.shape[4] // AVG
    for step in range(coarse_round):
        fine = pl.ds(step * AVG, AVG)
        for part in range(2):
            for spec in range(2):
                lanes = slice(spec * half, (spec + 1) * half)
                rows = pl.ds((2 * part + spec) * AVG, AVG)
                own_ref[turn * coarse_round + step, pair, rows, :] = jnp.concatenate(
                    [recv_ref[pair, turn, src, part, fine, lanes] for src in range(sources)],
                    axis=1,
                )


def exchange_kernel(
    parts,
    volt_ref,
    coef_ref,
    table_ref,
    out_ref,
    first_send,
    data_ref,
    rows_ref,
    filt_ref,
    mid_ref,
    send_ref,
    recv_ref,
    own_ref,
    first_send_sem,
    first_recv_sem,
    turn_send_sem,
    turn_recv_sem,
    keep_sem,
    row_send_sem,
    row_recv_sem,
    own_sem,
):
    mesh_id = pl.DeviceIdType.MESH
    me = lax.axis_index("ft")
    col = lax.axis_index("bl")
    mate = col + 1 - 2 * lax.rem(col, 2)
    across = lax.rem(col + 2, 4)
    pairs, rounds = send_ref.shape[:2]
    coarse_round = recv_ref.shape[4] // AVG

    barrier = pltpu.get_barrier_semaphore()
    for shift in range(1, parts):
        pl.semaphore_signal(
            barrier, inc=1, device_id={"ft": lax.rem(me + shift, parts)}, device_id_type=mesh_id
        )
    for peer in (mate, across):
        pl.semaphore_signal(barrier, inc=1, device_id={"bl": peer}, device_id_type=mesh_id)

    def first_copy(part, dest):
        place = lax.rem(dest - me + parts, parts) - 1
        return pltpu.make_async_remote_copy(
            src_ref=first_send.at[part, dest],
            dst_ref=data_ref.at[part, me],
            send_sem=first_send_sem.at[part, place],
            recv_sem=first_recv_sem.at[part, place],
            device_id={"ft": dest},
            device_id_type=mesh_id,
        )

    def turn_copy(pair, turn, dest):
        place = lax.rem(dest - me + parts, parts) - 1
        return pltpu.make_async_remote_copy(
            src_ref=send_ref.at[pair, turn, dest],
            dst_ref=recv_ref.at[pair, turn, me],
            send_sem=turn_send_sem.at[pair, turn, place],
            recv_sem=turn_recv_sem.at[pair, turn, place],
            device_id={"ft": dest},
            device_id_type=mesh_id,
        )

    first = []
    for part in range(HALVES):
        pack_half(part, volt_ref, first_send)
        if part == 0:
            pl.semaphore_wait(barrier, parts + 1)
        for rank in range(parts - 1):
            first_copy(part, far_first(me, parts, rank)).start()
        copies = [first_copy(part, lax.rem(me + shift, parts)) for shift in range(1, parts)]
        keep = pltpu.make_async_copy(first_send.at[part, me], data_ref.at[part, me], own_sem.at[part])
        keep.start()
        first.append((copies, keep))
    turn_coefs(coef_ref, rows_ref)

    def arrive(part):
        copies, keep = first[part]
        keep.wait()
        for copy in copies:
            copy.wait_recv()

    for part in range(HALVES - 1):
        arrive(part)
        for pair in range(pairs):
            filter_dft(pair, part, data_ref, rows_ref, table_ref, filt_ref, mid_ref)
    arrive(HALVES - 1)

    turn_copies = {}
    for pair in range(pairs):
        filter_dft(pair, HALVES - 1, data_ref, rows_ref, table_ref, filt_ref, mid_ref)
        radix_pass(pair, mid_ref, send_ref)
        for turn in range(rounds):
            for rank in range(parts - 1):
                turn_copy(pair, turn, far_first(me, parts, rank)).start()
            copies = [turn_copy(pair, turn, lax.rem(me + shift, parts)) for shift in range(1, parts)]
            keep = pltpu.make_async_copy(
                send_ref.at[pair, turn, me], recv_ref.at[pair, turn, me], keep_sem.at[pair, turn]
            )
            keep.start()
            turn_copies[pair, turn] = (copies, keep)

    def row_copy(kind, pair, turn, src, block, peer):
        rows = pl.ds(turn * coarse_round, coarse_round)
        return pltpu.make_async_remote_copy(
            src_ref=src,
            dst_ref=out_ref.at[block, rows, pair],
            send_sem=row_send_sem.at[kind, pair, turn],
            recv_sem=row_recv_sem.at[kind, pair, turn],
            device_id={"bl": peer},
            device_id_type=mesh_id,
        )

    order = [(pair, turn) for pair in range(pairs) for turn in range(rounds)]
    across_copies, late = {}, []

    def relay(pair, turn):
        across_copies[pair, turn].wait_recv()
        rows = pl.ds(turn * coarse_round, coarse_round)
        copy = row_copy(2, pair, turn, out_ref.at[across, rows, pair], across, mate)
        copy.start()
        late.append(copy)

    local = []
    lag = 3
    for count, (pair, turn) in enumerate(order):
        copies, keep = turn_copies[pair, turn]
        keep.wait()
        for copy in copies:
            copy.wait_recv()
        merge_round(pair, turn, recv_ref, own_ref)
        rows = pl.ds(turn * coarse_round, coarse_round)
        source = own_ref.at[rows, pair]
        far = row_copy(0, pair, turn, source, col, across)
        far.start()
        near = row_copy(1, pair, turn, source, col, mate)
        near.start()
        stay = pltpu.make_async_copy(source, out_ref.at[col, rows, pair], own_sem.at[HALVES + count])
        stay.start()
        across_copies[pair, turn] = far
        late.append(near)
        local.append(stay)
        if count >= lag:
            relay(*order[count - lag])
    for position in order[len(order) - lag :]:
        relay(*position)
    for copy in late:
        copy.wait()
    for copy in across_copies.values():
        copy.wait_send()
    for copy in local:
        copy.wait()
    for copies, _ in turn_copies.values():
        for copy in copies:
            copy.wait_send()
    for copies, _ in first:
        for copy in copies:
            copy.wait_send()


def exchange(voltages, coefs, table, parts, blocks):
    _, chan_count, rows_here = voltages.shape
    sub = chan_count // RADIX
    pairs = parts // 2
    rows_round = AVG
    rounds = RADIX // parts * (sub // rows_round)
    coarse_here = chan_count // parts // AVG
    depth = 4 * AVG
    vmem = pl.BlockSpec(memory_space=pltpu.VMEM)
    dma = pltpu.SemaphoreType.DMA
    return pl.pallas_call(
        functools.partial(exchange_kernel, parts),
        in_specs=[vmem] * 3,
        out_specs=pl.BlockSpec(memory_space=pl.ANY),
        out_shape=jax.ShapeDtypeStruct((blocks, coarse_here, pairs, depth, rows_here), jnp.bfloat16),
        scratch_shapes=[
            pltpu.VMEM((HALVES, parts, chan_count // HALVES, LANES), jnp.bfloat16),
            pltpu.VMEM((HALVES, parts, chan_count // HALVES, LANES), jnp.bfloat16),
            pltpu.VMEM((HALVES, chan_count // HALVES, coefs.shape[0]), jnp.float32),
            pltpu.VMEM((2, chan_count // HALVES, LANES), jnp.float32),
            pltpu.VMEM((pairs, RADIX, 2 * sub, LANES), jnp.float32),
            pltpu.VMEM((pairs, rounds, parts, 2, rows_round, LANES), jnp.bfloat16),
            pltpu.VMEM((pairs, rounds, parts, 2, rows_round, LANES), jnp.bfloat16),
            pltpu.VMEM((coarse_here, pairs, depth, rows_here), jnp.bfloat16),
            dma((HALVES, parts - 1)),
            dma((HALVES, parts - 1)),
            dma((pairs, rounds, parts - 1)),
            dma((pairs, rounds, parts - 1)),
            dma((pairs, rounds)),
            dma((3, pairs, rounds)),
            dma((3, pairs, rounds)),
            dma((HALVES + pairs * rounds,)),
        ],
        compiler_params=pltpu.CompilerParams(collective_id=0, has_side_effects=True),
        name="exchange",
    )(voltages, coefs, table)


def plan_slots(ids_ref, owner_ref, slot_ref, blocks):
    my_index = lax.axis_index("bl")
    slot_cap = slot_ref.shape[1]
    for slot in range(slot_cap):
        for row in range(3):
            slot_ref[row, slot] = 0
    shard_of = []
    for label in range(blocks):
        shard = jnp.int32(0)
        for pos in range(blocks):
            shard = shard + jnp.where(ids_ref[pos] == label, pos, 0)
        shard_of.append(shard)
    count = jnp.int32(0)
    pairs = [(i, j) for i in range(blocks) for j in range(i, blocks)]
    for tile, (first_id, second_id) in enumerate(pairs):
        mine = (owner_ref[tile] == my_index) & (count < slot_cap)

        @pl.when(mine)
        def _():
            slot_ref[0, count] = shard_of[first_id]
            slot_ref[1, count] = shard_of[second_id]
            slot_ref[2, count] = 1

        count = count + mine.astype(jnp.int32)


def tiles_kernel(norm_scale, ids_ref, owner_ref, data_ref, out_ref, slot_ref):
    blocks, _, pairs, depth, rows_here = data_ref.shape

    @pl.when(pl.program_id(0) == 0)
    def _():
        plan_slots(ids_ref, owner_ref, slot_ref, blocks)

    for slot in range(out_ref.shape[2]):
        used = slot_ref[2, slot] > 0

        @pl.when(used)
        def _():
            row = data_ref[slot_ref[0, slot], 0].reshape(pairs * depth, rows_here)
            col = data_ref[slot_ref[1, slot], 0].reshape(pairs * depth, rows_here)
            turned = jnp.transpose(row)
            half = depth // 2
            pieces = [turned[:, pos * half : (pos + 1) * half] for pos in range(2 * pairs)]
            swapped = jnp.concatenate(
                [-pieces[pos - 1] if pos % 2 else pieces[pos + 1] for pos in range(2 * pairs)], axis=1
            )
            real = jnp.dot(turned, col, preferred_element_type=jnp.float32)
            out_ref[0, 0, slot] = real * norm_scale
            imag = jnp.dot(swapped, col, preferred_element_type=jnp.float32)
            out_ref[1, 0, slot] = imag * norm_scale

        @pl.when(jnp.logical_not(used))
        def _():
            out_ref[0, 0, slot] = jnp.zeros(out_ref.shape[3:], jnp.float32)
            out_ref[1, 0, slot] = jnp.zeros(out_ref.shape[3:], jnp.float32)


def make_tiles(block_ids, tile_owner, gathered, norm_scale):
    blocks, coarse_here, pairs, depth, rows_here = gathered.shape
    tile_count = blocks * (blocks + 1) // 2
    slot_cap = 2 * tile_count // blocks
    return pl.pallas_call(
        functools.partial(tiles_kernel, norm_scale),
        grid_spec=pltpu.PrefetchScalarGridSpec(
            num_scalar_prefetch=2,
            grid=(coarse_here,),
            in_specs=[
                pl.BlockSpec(
                    (blocks, 1, pairs, depth, rows_here), lambda c, *_: (0, c, 0, 0, 0)
                )
            ],
            out_specs=pl.BlockSpec(
                (2, 1, slot_cap, rows_here, rows_here), lambda c, *_: (0, c, 0, 0, 0)
            ),
            scratch_shapes=[pltpu.SMEM((3, slot_cap), jnp.int32)],
        ),
        out_shape=jax.ShapeDtypeStruct((2, coarse_here, slot_cap, rows_here, rows_here), jnp.float32),
        name="tiles",
    )(block_ids, tile_owner, gathered)


def per_device_packed(voltages, coefs, block_ids, tile_owner):
    parts = lax.axis_size("ft")
    table = jnp.asarray(dft_constants(coefs.shape[1]))
    gathered = exchange(voltages, coefs, table, parts, lax.axis_size("bl"))
    return make_tiles(block_ids, tile_owner, gathered, 1.0 / (AVG * parts))


def per_device(voltages, coefs, block_ids, tile_owner):
    chan_count = coefs.shape[1]
    parts = lax.axis_size("ft")
    fits = (
        voltages.shape[1] == chan_count
        and parts % 2 == 0
        and RADIX % parts == 0
        and voltages.shape[2] == parts * LANES // 2
        and chan_count == RADIX * LANES
        and (chan_count // RADIX) % AVG == 0
        and lax.axis_size("bl") == 4
    )
    if fits:
        return per_device_packed(voltages, coefs, block_ids, tile_owner)
    return per_device_general(voltages, coefs, block_ids, tile_owner)


def solution(mesh):
    return jax.shard_map(
        per_device,
        mesh=mesh,
        in_specs=(P(None, ("grp", "ft"), "bl"), P(), P(), P("grp")),
        out_specs=P(None, ("grp", "ft"), "bl", None, None),
        check_vma=False,
    )
```

profile of v0, /device:TPU:1, one launch (start us, length us, event | category | flops | bytes accessed | tf_op | source)
XLA Modules:
  0.0 137.6 jit_solution(7677269948881123833)
XLA Ops:
  0.0 119.4 %exchange.1.data_ref = bf16[4,8,2,256,256]{4,3,2,1,0:T(8,128)(2,1)} custom-call(bf16[2,2048,256]{2,1,0:T(8,128)(2,1)} %volt_ref.1, f32[8,2048]{1,0:T(8,128)} %coef_ref.1, bf16[16,4,128,128]{3,2,1,0:T(8,128)(2,1)} %constant.2.clone.table_ref), custom_call_target="tpu_custom_call" | custom-call | tf_op jit(solution)/shard_map/exchange/pallas_call | solution.py:530
  119.4 18.2 %tiles.1 = f32[2,8,5,256,256]{4,3,2,1,0:T(8,128)} custom-call(s32[4]{0:T(128)} %ids_ref.1, s32[10]{0:T(128)} %owner_ref.1, bf16[4,8,2,256,256]{4,3,2,1,0:T(8,128)(2,1)} %exchange.1.data_ref), custom_call_target="tpu_custom_call" | custom-call | tf_op jit(solution)/shard_map/tiles/pallas_call | solution.py:619
where the time goes:
time: 138 us
  Pallas kernels  138 us (100%)
    pallas_call x1, Pallas kernels, exchange(): pl.pallas_call(functools.partial(exchange_kernel, parts), in_specs=[vmem]...  119 us
    pallas_call x1, Pallas kernels, make_tiles(): pl.pallas_call(functools.partial(tiles_kernel, norm_scale), grid_spec=plt...  18.2 us

commit v1 on v0

--- a/solution.py
+++ b/solution.py
@@ -152,6 +152,7 @@
 
 LANES = 128
 RADIX = 16
+WINDOW = 2
 
 
 def split_halves(values):
@@ -343,20 +344,24 @@
         lax.fori_loop(0, rows_round // rows_step, radix_step, 0)
 
 
-def merge_round(pair, turn, recv_ref, own_ref):
+def merge_round(pair, turn, col, recv_ref, out_ref):
     half = LANES // 2
     sources = recv_ref.shape[2]
     coarse_round = recv_ref.shape[4] // AVG
     for step in range(coarse_round):
         fine = pl.ds(step * AVG, AVG)
+        rows = []
         for part in range(2):
             for spec in range(2):
                 lanes = slice(spec * half, (spec + 1) * half)
-                rows = pl.ds((2 * part + spec) * AVG, AVG)
-                own_ref[turn * coarse_round + step, pair, rows, :] = jnp.concatenate(
-                    [recv_ref[pair, turn, src, part, fine, lanes] for src in range(sources)],
-                    axis=1,
+                rows.append(
+                    jnp.concatenate(
+                        [recv_ref[pair, turn, src, part, fine, lanes] for src in range(sources)],
+                        axis=1,
+                    )
                 )
+        merged = jnp.concatenate(rows, axis=0)
+        out_ref[col, turn * coarse_round + step, pair] = jnp.transpose(merged)
 
 
 def exchange_kernel(
@@ -372,7 +377,6 @@
     mid_ref,
     send_ref,
     recv_ref,
-    own_ref,
     first_send_sem,
     first_recv_sem,
     turn_send_sem,
@@ -446,12 +450,17 @@
     arrive(HALVES - 1)
 
     turn_copies = {}
+
+    def send_turn(pair, turn):
+        for rank in range(parts - 1):
+            turn_copy(pair, turn, far_first(me, parts, rank)).start()
+
     for pair in range(pairs):
         filter_dft(pair, HALVES - 1, data_ref, rows_ref, table_ref, filt_ref, mid_ref)
         radix_pass(pair, mid_ref, send_ref)
         for turn in range(rounds):
-            for rank in range(parts - 1):
-                turn_copy(pair, turn, far_first(me, parts, rank)).start()
+            if pair * rounds + turn < WINDOW:
+                send_turn(pair, turn)
             copies = [turn_copy(pair, turn, lax.rem(me + shift, parts)) for shift in range(1, parts)]
             keep = pltpu.make_async_copy(
                 send_ref.at[pair, turn, me], recv_ref.at[pair, turn, me], keep_sem.at[pair, turn]
@@ -480,25 +489,23 @@
         copy.start()
         late.append(copy)
 
-    local = []
     lag = 3
     for count, (pair, turn) in enumerate(order):
         copies, keep = turn_copies[pair, turn]
         keep.wait()
         for copy in copies:
             copy.wait_recv()
-        merge_round(pair, turn, recv_ref, own_ref)
+        if count + WINDOW < len(order):
+            send_turn(*order[count + WINDOW])
+        merge_round(pair, turn, col, recv_ref, out_ref)
         rows = pl.ds(turn * coarse_round, coarse_round)
-        source = own_ref.at[rows, pair]
+        source = out_ref.at[col, rows, pair]
         far = row_copy(0, pair, turn, source, col, across)
         far.start()
         near = row_copy(1, pair, turn, source, col, mate)
         near.start()
-        stay = pltpu.make_async_copy(source, out_ref.at[col, rows, pair], own_sem.at[HALVES + count])
-        stay.start()
         across_copies[pair, turn] = far
         late.append(near)
-        local.append(stay)
         if count >= lag:
             relay(*order[count - lag])
     for position in order[len(order) - lag :]:
@@ -507,8 +514,6 @@
         copy.wait()
     for copy in across_copies.values():
         copy.wait_send()
-    for copy in local:
-        copy.wait()
     for copies, _ in turn_copies.values():
         for copy in copies:
             copy.wait_send()
@@ -530,8 +535,8 @@
     return pl.pallas_call(
         functools.partial(exchange_kernel, parts),
         in_specs=[vmem] * 3,
-        out_specs=pl.BlockSpec(memory_space=pl.ANY),
-        out_shape=jax.ShapeDtypeStruct((blocks, coarse_here, pairs, depth, rows_here), jnp.bfloat16),
+        out_specs=vmem,
+        out_shape=pltpu.VMEM((blocks, coarse_here, pairs, rows_here, depth), jnp.bfloat16),
         scratch_shapes=[
             pltpu.VMEM((HALVES, parts, chan_count // HALVES, LANES), jnp.bfloat16),
             pltpu.VMEM((HALVES, parts, chan_count // HALVES, LANES), jnp.bfloat16),
@@ -540,7 +545,6 @@
             pltpu.VMEM((pairs, RADIX, 2 * sub, LANES), jnp.float32),
             pltpu.VMEM((pairs, rounds, parts, 2, rows_round, LANES), jnp.bfloat16),
             pltpu.VMEM((pairs, rounds, parts, 2, rows_round, LANES), jnp.bfloat16),
-            pltpu.VMEM((coarse_here, pairs, depth, rows_here), jnp.bfloat16),
             dma((HALVES, parts - 1)),
             dma((HALVES, parts - 1)),
             dma((pairs, rounds, parts - 1)),
@@ -548,9 +552,11 @@
             dma((pairs, rounds)),
             dma((3, pairs, rounds)),
             dma((3, pairs, rounds)),
-            dma((HALVES + pairs * rounds,)),
+            dma((HALVES,)),
         ],
-        compiler_params=pltpu.CompilerParams(collective_id=0, has_side_effects=True),
+        compiler_params=pltpu.CompilerParams(
+            collective_id=0, has_side_effects=True, vmem_limit_bytes=40 * 2**20
+        ),
         name="exchange",
     )(voltages, coefs, table)
 
@@ -582,38 +588,32 @@
 
 
 def tiles_kernel(norm_scale, ids_ref, owner_ref, data_ref, out_ref, slot_ref):
-    blocks, _, pairs, depth, rows_here = data_ref.shape
-
-    @pl.when(pl.program_id(0) == 0)
+    _, _, pairs, _, depth = data_ref.shape
+    coarse = pl.program_id(0)
+
+    @pl.when(coarse == 0)
     def _():
-        plan_slots(ids_ref, owner_ref, slot_ref, blocks)
-
+        plan_slots(ids_ref, owner_ref, slot_ref, data_ref.shape[0])
+
+    half = depth // 2
+    contract = (((1,), (1,)), ((), ()))
     for slot in range(out_ref.shape[2]):
-        used = slot_ref[2, slot] > 0
-
-        @pl.when(used)
-        def _():
-            row = data_ref[slot_ref[0, slot], 0].reshape(pairs * depth, rows_here)
-            col = data_ref[slot_ref[1, slot], 0].reshape(pairs * depth, rows_here)
-            turned = jnp.transpose(row)
-            half = depth // 2
-            pieces = [turned[:, pos * half : (pos + 1) * half] for pos in range(2 * pairs)]
-            swapped = jnp.concatenate(
-                [-pieces[pos - 1] if pos % 2 else pieces[pos + 1] for pos in range(2 * pairs)], axis=1
-            )
-            real = jnp.dot(turned, col, preferred_element_type=jnp.float32)
-            out_ref[0, 0, slot] = real * norm_scale
-            imag = jnp.dot(swapped, col, preferred_element_type=jnp.float32)
-            out_ref[1, 0, slot] = imag * norm_scale
-
-        @pl.when(jnp.logical_not(used))
-        def _():
-            out_ref[0, 0, slot] = jnp.zeros(out_ref.shape[3:], jnp.float32)
-            out_ref[1, 0, slot] = jnp.zeros(out_ref.shape[3:], jnp.float32)
+        scale = jnp.where(slot_ref[2, slot] > 0, norm_scale, 0.0)
+        real, imag = None, None
+        for pair in range(pairs):
+            row = data_ref[slot_ref[0, slot], coarse, pair]
+            col = data_ref[slot_ref[1, slot], coarse, pair]
+            swapped = jnp.concatenate([row[:, half:], -row[:, :half]], axis=1)
+            first = lax.dot_general(row, col, contract, preferred_element_type=jnp.float32)
+            second = lax.dot_general(swapped, col, contract, preferred_element_type=jnp.float32)
+            real = first if real is None else real + first
+            imag = second if imag is None else imag + second
+        out_ref[0, 0, slot] = real * scale
+        out_ref[1, 0, slot] = imag * scale
 
 
 def make_tiles(block_ids, tile_owner, gathered, norm_scale):
-    blocks, coarse_here, pairs, depth, rows_here = gathered.shape
+    blocks, coarse_here, pairs, rows_here, depth = gathered.shape
     tile_count = blocks * (blocks + 1) // 2
     slot_cap = 2 * tile_count // blocks
     return pl.pallas_call(
@@ -621,17 +621,14 @@
         grid_spec=pltpu.PrefetchScalarGridSpec(
             num_scalar_prefetch=2,
             grid=(coarse_here,),
-            in_specs=[
-                pl.BlockSpec(
-                    (blocks, 1, pairs, depth, rows_here), lambda c, *_: (0, c, 0, 0, 0)
-                )
-            ],
+            in_specs=[pl.BlockSpec(memory_space=pltpu.VMEM)],
             out_specs=pl.BlockSpec(
                 (2, 1, slot_cap, rows_here, rows_here), lambda c, *_: (0, c, 0, 0, 0)
             ),
             scratch_shapes=[pltpu.SMEM((3, slot_cap), jnp.int32)],
         ),
         out_shape=jax.ShapeDtypeStruct((2, coarse_here, slot_cap, rows_here, rows_here), jnp.float32),
+        compiler_params=pltpu.CompilerParams(vmem_limit_bytes=40 * 2**20),
         name="tiles",
     )(block_ids, tile_owner, gathered)
 

time: 138 us -> 124 us (0.90)
  Pallas kernels: 138 us -> 120 us
  local copies, waits for them, and re-layouts: 0 us -> 4.03 us
    pallas_call x1, Pallas kernels: 119 us -> 109 us  [exchange(): pl.pallas_call(functools.partial(exchange_kernel, parts), in_specs=[vmem]...]
    pallas_call x1, Pallas kernels: 18.2 us -> 11 us  [make_tiles(): pl.pallas_call(functools.partial(tiles_kernel, norm_scale), grid_spec=plt...]
    unnamed x0 -> x10, local copies, waits for them, and re-layouts: none -> 4.03 us
where the time goes in v1:
time: 124 us
  Pallas kernels  120 us (97%)
  local copies, waits for them, and re-layouts  4.03 us (3%)
    pallas_call x1, Pallas kernels, exchange(): pl.pallas_call(functools.partial(exchange_kernel, parts), in_specs=[vmem]...  109 us
    pallas_call x1, Pallas kernels, make_tiles(): pl.pallas_call(functools.partial(tiles_kernel, norm_scale), grid_spec=plt...  11 us
    unnamed x10, local copies, waits for them, and re-layouts  4.03 us

profile of v1, /device:TPU:1, one launch (start us, length us, event | category | flops | bytes accessed | tf_op | source)
XLA Modules:
  0.0 123.8 jit_solution(8398575327622969528)
XLA Ops:
  0.0 0.0 copy-start
  0.0 1.6 %copy-done = bf16[2,2048,256]{2,1,0:T(8,128)(2,1)S(1)} copy-done((bf16[2,2048,256]{2,1,0:T(8,128)(2,1)S(1)}, bf16[2,2048,256]{2,1,0:T(8,128)(2,1)}, u32[]{:S(2)}) %copy-start) | copy-done | bytes 2097176
  1.6 0.0 copy-start.1
  1.6 1.6 %copy-done.1 = bf16[16,4,128,128]{3,2,1,0:T(8,128)(2,1)S(1)} copy-done((bf16[16,4,128,128]{3,2,1,0:T(8,128)(2,1)S(1)}, bf16[16,4,128,128]{3,2,1,0:T(8,128)(2,1)}, u32[]{:S(2)}) %copy-start.1) | copy-done | bytes 2097176
  3.2 0.0 copy-start.2
  3.2 0.8 copy-done.2
  4.0 0.0 copy-start.3
  4.0 0.0 copy-start.4
  4.0 108.8 %exchange.1.data_ref = bf16[4,8,2,256,256]{4,3,2,1,0:T(8,128)(2,1)S(1)} custom-call(bf16[2,2048,256]{2,1,0:T(8,128)(2,1)S(1)} %copy-done, f32[8,2048]{1,0:T(8,128)S(1)} %copy-done.2, bf16[16,4,128,128]{3,2,1,0:T(8,128)(2,1)S(1)} %copy-done.1), custom_call_target="tpu_custom_call" | custom-call | tf_op jit(solution)/shard_map/exchange/pallas_call | solution.py:535
  112.8 0.0 copy-done.3
  112.8 0.0 copy-done.4
  112.8 11.0 %tiles.1 = f32[2,8,5,256,256]{4,3,2,1,0:T(8,128)} custom-call(s32[4]{0:T(128)S(1)} %copy-done.3, s32[10]{0:T(128)S(1)} %copy-done.4, bf16[4,8,2,256,256]{4,3,2,1,0:T(8,128)(2,1)S(1)} %exchange.1.data_ref), custom_call_target="tpu_custom_call" | custom-call | tf_op jit(solution)/shard_map/tiles/pallas_call | solution.py:619
Async XLA Ops:
  0.0 1.6 %copy-start = (bf16[2,2048,256]{2,1,0:T(8,128)(2,1)S(1)}, bf16[2,2048,256]{2,1,0:T(8,128)(2,1)}, u32[]{:S(2)}) copy-start(bf16[2,2048,256]{2,1,0:T(8,128)(2,1)} %volt_ref.1) | copy-start | bytes 6291460
  1.6 1.6 %copy-start.1 = (bf16[16,4,128,128]{3,2,1,0:T(8,128)(2,1)S(1)}, bf16[16,4,128,128]{3,2,1,0:T(8,128)(2,1)}, u32[]{:S(2)}) copy-start(bf16[16,4,128,128]{3,2,1,0:T(8,128)(2,1)} %constant.2.clone.table_ref) | copy-start | bytes 6291460
  3.2 0.8 copy-start.2
  4.0 108.8 %copy-start.3 = (s32[4]{0:T(128)S(1)}, s32[4]{0:T(128)}, u32[]{:S(2)}) copy-start(s32[4]{0:T(128)} %ids_ref.1) | copy-start | bytes 52
  4.0 108.8 %copy-start.4 = (s32[10]{0:T(128)S(1)}, s32[10]{0:T(128)}, u32[]{:S(2)}) copy-start(s32[10]{0:T(128)} %owner_ref.1) | copy-start | bytes 124

commit v2 on v1

--- a/solution.py
+++ b/solution.py
@@ -152,7 +152,9 @@
 
 LANES = 128
 RADIX = 16
-WINDOW = 2
+WINDOW = 3
+LAG = 3
+SPARE = 4
 
 
 def split_halves(values):
@@ -209,32 +211,28 @@
     return first + second
 
 
-HALVES = 2
-SUBROWS = RADIX // HALVES
-
-
-def pick_half(values, part):
-    rows, lanes = values.shape
-    return values.reshape(rows // RADIX, HALVES, SUBROWS, lanes)[:, part].reshape(-1, lanes)
-
-
-def pack_half(part, volt_ref, first_send):
-    half = LANES // 2
-    block = 256
+CHUNKS = 2
+SPECTRA = 4
+GROUP = LANES // SPECTRA
+
+
+def pack_chunk(chunk, volt_ref, first_send):
+    rows_half = first_send.shape[2]
+    tile = slice(chunk * LANES, (chunk + 1) * LANES)
+    block = 64
 
     def step(pos, carry):
         rows = pl.ds(pl.multiple_of(pos * block, block), block)
-        out_rows = pl.ds(pl.multiple_of(pos * (block // HALVES), block // HALVES), block // HALVES)
+        late = pl.ds(pl.multiple_of(rows_half + pos * block, block), block)
+        pieces = [volt_ref[part, place, tile] for place in (rows, late) for part in range(2)]
         for dest in range(first_send.shape[1]):
-            lanes = slice(dest * half, (dest + 1) * half)
-            real = pick_half(volt_ref[0, rows, lanes].astype(jnp.float32), part)
-            imag = pick_half(volt_ref[1, rows, lanes].astype(jnp.float32), part)
-            first_send[part, dest, out_rows, :] = jnp.concatenate([real, imag], axis=1).astype(
-                first_send.dtype
+            lanes = slice(dest * GROUP, (dest + 1) * GROUP)
+            first_send[chunk, dest, rows, :] = jnp.concatenate(
+                [piece[:, lanes] for piece in pieces], axis=1
             )
         return carry
 
-    lax.fori_loop(0, volt_ref.shape[1] // block, step, 0)
+    lax.fori_loop(0, rows_half // block, step, 0)
 
 
 def far_first(me, parts, rank):
@@ -244,59 +242,83 @@
     return jnp.where(me < parts // 2, down, up)
 
 
-def turn_coefs(coef_ref, rows_ref):
-    block = 256
+def widen_coefs(coef_ref, wide_ref):
+    taps_count = coef_ref.shape[0]
+    lags, rows_half, _ = wide_ref.shape
+    block = 128
 
     def step(pos, carry):
-        lanes = pl.ds(pl.multiple_of(pos * block, block), block)
-        out_rows = pl.ds(pl.multiple_of(pos * (block // HALVES), block // HALVES), block // HALVES)
-        turned = jnp.transpose(coef_ref[:, lanes])
-        for part in range(HALVES):
-            rows_ref[part, out_rows, :] = pick_half(turned, part)
+        rows = pl.ds(pl.multiple_of(pos * block, block), block)
+        late = pl.ds(pl.multiple_of(rows_half + pos * block, block), block)
+        first = jnp.transpose(coef_ref[:, rows])
+        second = jnp.transpose(coef_ref[:, late])
+        low_lane = lax.broadcasted_iota(jnp.int32, (block, LANES), 1) < LANES // 2
+        for lag in range(lags):
+            tap = taps_count - 1 - lag
+            wide_ref[lag, rows, :] = jnp.where(
+                low_lane, first[:, tap : tap + 1], second[:, tap : tap + 1]
+            )
         return carry
 
-    lax.fori_loop(0, coef_ref.shape[1] // block, step, 0)
-
-
-def filter_dft(pair, part, data_ref, rows_ref, table_ref, filt_ref, mid_ref):
-    taps_count = rows_ref.shape[2]
+    lax.fori_loop(0, rows_half // block, step, 0)
+
+
+def swap_groups(values):
+    lane = lax.broadcasted_iota(jnp.int32, values[0].shape, 1)
+    low = lane < 2 * GROUP
+    even = lane % (2 * GROUP) < GROUP
+    mixed = [None] * 4
+    for pos in range(2):
+        one, two = values[pos], values[pos + 2]
+        mixed[pos] = jnp.where(low, one, pltpu.roll(two, 2 * GROUP, 1))
+        mixed[pos + 2] = jnp.where(low, pltpu.roll(one, 2 * GROUP, 1), two)
+    result = [None] * 4
+    for pos in (0, 2):
+        one, two = mixed[pos], mixed[pos + 1]
+        result[pos] = jnp.where(even, one, pltpu.roll(two, GROUP, 1))
+        result[pos + 1] = jnp.where(even, pltpu.roll(one, 3 * GROUP, 1), two)
+    return result
+
+
+def filter_chunk(chunk, first, count, data_ref, wide_ref, filt_ref):
+    lags = wide_ref.shape[0]
     rows_half = data_ref.shape[2]
-    sub = rows_half // SUBROWS
-    half = LANES // 2
-    block = 128
-
-    def filter_step(step, carry):
-        rows = pl.ds(pl.multiple_of(step * block, block), block)
-        coef = rows_ref[part, rows, :]
-        low_lane = lax.broadcasted_iota(jnp.int32, (block, LANES), 1) < half
-        samples = {}
-        for time_pos in range(max(0, 2 * pair - taps_count + 1), 2 * pair + 2):
-            samples[time_pos] = data_ref[part, time_pos, rows, :].astype(jnp.float32)
+    block = 16
+
+    def step(pos, carry):
+        rows = pl.ds(pl.multiple_of(pos * block, block), block)
+        late = pl.ds(pl.multiple_of(rows_half + pos * block, block), block)
+        samples = [data_ref[chunk, src, rows, :].astype(jnp.float32) for src in range(SPECTRA)]
+        coef = [wide_ref[lag, rows, :] for lag in range(lags)]
         sums = []
-        for spectrum in (2 * pair, 2 * pair + 1):
+        for spectrum in range(SPECTRA):
             total = None
-            for tap in range(taps_count):
-                time_pos = spectrum - (taps_count - 1) + tap
-                if time_pos < 0:
-                    continue
-                term = coef[:, tap : tap + 1] * samples[time_pos]
+            for time_pos in range(max(0, spectrum - lags + 1), spectrum + 1):
+                term = coef[spectrum - time_pos] * samples[time_pos]
                 total = term if total is None else total + term
             sums.append(total)
-        filt_ref[0, rows, :] = jnp.where(low_lane, sums[0], pltpu.roll(sums[1], half, 1))
-        filt_ref[1, rows, :] = jnp.where(low_lane, pltpu.roll(sums[0], half, 1), sums[1])
+        re_first, im_first, re_late, im_late = swap_groups(sums)
+        filt_ref[0, rows, :] = re_first
+        filt_ref[1, rows, :] = im_first
+        filt_ref[0, late, :] = re_late
+        filt_ref[1, late, :] = im_late
         return carry
 
-    lax.fori_loop(0, rows_half // block, filter_step, 0)
-
-    def dft_step(offset, carry):
-        phase = part * SUBROWS + offset
-        real_in = filt_ref[0, pl.ds(offset, sub, stride=SUBROWS), :]
-        imag_in = filt_ref[1, pl.ds(offset, sub, stride=SUBROWS), :]
+    lax.fori_loop(first // block, (first + count) // block, step, 0, unroll=2)
+
+
+def dft_chunk(chunk, first, count, table_ref, filt_ref, mid_ref):
+    sub = filt_ref.shape[1] // RADIX
+
+    def dft_step(step, carry):
+        phase = first + step
+        real_in = filt_ref[0, pl.ds(phase, sub, stride=RADIX), :]
+        imag_in = filt_ref[1, pl.ds(phase, sub, stride=RADIX), :]
         high, low = split_halves(jnp.concatenate([real_in, imag_in], axis=0))
 
-        def matrix(first):
-            cos_m = table_ref[phase, first]
-            sin_m = table_ref[phase, first + 1]
+        def matrix(pick):
+            cos_m = table_ref[phase, pick]
+            sin_m = table_ref[phase, pick + 1]
             return jnp.concatenate(
                 [
                     jnp.concatenate([cos_m, sin_m], axis=1),
@@ -309,13 +331,13 @@
         total = jnp.dot(big, low, preferred_element_type=jnp.float32)
         total = total + jnp.dot(small, high, preferred_element_type=jnp.float32)
         total = total + jnp.dot(big, high, preferred_element_type=jnp.float32)
-        mid_ref[pair, phase] = total
+        mid_ref[chunk, phase] = total
         return carry
 
-    lax.fori_loop(0, SUBROWS, dft_step, 0, unroll=4)
-
-
-def radix_pass(pair, mid_ref, send_ref):
+    lax.fori_loop(0, count, dft_step, 0, unroll=4)
+
+
+def radix_pass(chunk, mid_ref, send_ref):
     rounds, parts = send_ref.shape[1:3]
     rows_round = send_ref.shape[4]
     sub = mid_ref.shape[2] // 2
@@ -330,53 +352,51 @@
             start = pl.multiple_of(split * rows_round + step * rows_step, rows_step)
             values = [
                 (
-                    mid_ref[pair, phase, pl.ds(start, rows_step), :],
-                    mid_ref[pair, phase, pl.ds(sub + start, rows_step), :],
+                    mid_ref[chunk, phase, pl.ds(start, rows_step), :],
+                    mid_ref[chunk, phase, pl.ds(sub + start, rows_step), :],
                 )
                 for phase in range(RADIX)
             ]
             for group, (re, im) in enumerate(small_fft(values)):
                 dest, turn = group // groups, group % groups * splits + split
-                send_ref[pair, turn, dest, 0, out_rows, :] = re.astype(jnp.bfloat16)
-                send_ref[pair, turn, dest, 1, out_rows, :] = im.astype(jnp.bfloat16)
+                send_ref[chunk, turn, dest, 0, out_rows, :] = re.astype(jnp.bfloat16)
+                send_ref[chunk, turn, dest, 1, out_rows, :] = im.astype(jnp.bfloat16)
             return carry
 
         lax.fori_loop(0, rows_round // rows_step, radix_step, 0)
 
 
-def merge_round(pair, turn, col, recv_ref, out_ref):
-    half = LANES // 2
-    sources = recv_ref.shape[2]
+def merge_round(chunk, turn, col, recv_ref, out_ref):
     coarse_round = recv_ref.shape[4] // AVG
     for step in range(coarse_round):
         fine = pl.ds(step * AVG, AVG)
-        rows = []
-        for part in range(2):
-            for spec in range(2):
-                lanes = slice(spec * half, (spec + 1) * half)
-                rows.append(
-                    jnp.concatenate(
-                        [recv_ref[pair, turn, src, part, fine, lanes] for src in range(sources)],
-                        axis=1,
-                    )
-                )
-        merged = jnp.concatenate(rows, axis=0)
-        out_ref[col, turn * coarse_round + step, pair] = jnp.transpose(merged)
+        for src in range(recv_ref.shape[2]):
+            both = [recv_ref[chunk, turn, src, part, fine, :] for part in range(2)]
+            turned = jnp.transpose(jnp.concatenate(both, axis=0))
+            for spectrum in range(SPECTRA):
+                depth = pl.ds(spectrum * 2 * AVG, 2 * AVG)
+                out_ref[
+                    col, turn * coarse_round + step, chunk, pl.ds(src * GROUP, GROUP), depth
+                ] = turned[spectrum * GROUP : (spectrum + 1) * GROUP]
 
 
 def exchange_kernel(
     parts,
+    volt_in,
+    coef_in,
+    table_in,
+    out_ref,
     volt_ref,
     coef_ref,
     table_ref,
-    out_ref,
     first_send,
     data_ref,
-    rows_ref,
+    wide_ref,
     filt_ref,
     mid_ref,
     send_ref,
     recv_ref,
+    load_sem,
     first_send_sem,
     first_recv_sem,
     turn_send_sem,
@@ -391,7 +411,7 @@
     col = lax.axis_index("bl")
     mate = col + 1 - 2 * lax.rem(col, 2)
     across = lax.rem(col + 2, 4)
-    pairs, rounds = send_ref.shape[:2]
+    rounds = send_ref.shape[1]
     coarse_round = recv_ref.shape[4] // AVG
 
     barrier = pltpu.get_barrier_semaphore()
@@ -402,113 +422,144 @@
     for peer in (mate, across):
         pl.semaphore_signal(barrier, inc=1, device_id={"bl": peer}, device_id_type=mesh_id)
 
-    def first_copy(part, dest):
+    volt_loads = []
+    for chunk in range(CHUNKS):
+        tile = pl.ds(chunk * LANES, LANES)
+        volt_loads.append(
+            pltpu.make_async_copy(
+                volt_in.at[:, :, tile], volt_ref.at[:, :, tile], load_sem.at[chunk]
+            )
+        )
+    coef_load = pltpu.make_async_copy(coef_in, coef_ref, load_sem.at[CHUNKS])
+    table_load = pltpu.make_async_copy(table_in, table_ref, load_sem.at[CHUNKS + 1])
+    for copy in (*volt_loads, coef_load, table_load):
+        copy.start()
+
+    def first_copy(chunk, dest):
         place = lax.rem(dest - me + parts, parts) - 1
         return pltpu.make_async_remote_copy(
-            src_ref=first_send.at[part, dest],
-            dst_ref=data_ref.at[part, me],
-            send_sem=first_send_sem.at[part, place],
-            recv_sem=first_recv_sem.at[part, place],
+            src_ref=first_send.at[chunk, dest],
+            dst_ref=data_ref.at[chunk, me],
+            send_sem=first_send_sem.at[chunk, place],
+            recv_sem=first_recv_sem.at[chunk, place],
             device_id={"ft": dest},
             device_id_type=mesh_id,
         )
 
-    def turn_copy(pair, turn, dest):
+    def turn_copy(chunk, turn, dest):
         place = lax.rem(dest - me + parts, parts) - 1
         return pltpu.make_async_remote_copy(
-            src_ref=send_ref.at[pair, turn, dest],
-            dst_ref=recv_ref.at[pair, turn, me],
-            send_sem=turn_send_sem.at[pair, turn, place],
-            recv_sem=turn_recv_sem.at[pair, turn, place],
+            src_ref=send_ref.at[chunk, turn, dest],
+            dst_ref=recv_ref.at[chunk, turn, me],
+            send_sem=turn_send_sem.at[chunk, turn, place],
+            recv_sem=turn_recv_sem.at[chunk, turn, place],
             device_id={"ft": dest},
             device_id_type=mesh_id,
         )
 
     first = []
-    for part in range(HALVES):
-        pack_half(part, volt_ref, first_send)
-        if part == 0:
+    for chunk in range(CHUNKS):
+        volt_loads[chunk].wait()
+        pack_chunk(chunk, volt_ref, first_send)
+        if chunk == 0:
             pl.semaphore_wait(barrier, parts + 1)
         for rank in range(parts - 1):
-            first_copy(part, far_first(me, parts, rank)).start()
-        copies = [first_copy(part, lax.rem(me + shift, parts)) for shift in range(1, parts)]
-        keep = pltpu.make_async_copy(first_send.at[part, me], data_ref.at[part, me], own_sem.at[part])
+            first_copy(chunk, far_first(me, parts, rank)).start()
+        copies = [first_copy(chunk, lax.rem(me + shift, parts)) for shift in range(1, parts)]
+        keep = pltpu.make_async_copy(
+            first_send.at[chunk, me], data_ref.at[chunk, me], own_sem.at[chunk]
+        )
         keep.start()
         first.append((copies, keep))
-    turn_coefs(coef_ref, rows_ref)
-
-    def arrive(part):
-        copies, keep = first[part]
+    coef_load.wait()
+    widen_coefs(coef_ref, wide_ref)
+    table_load.wait()
+
+    def arrive(chunk):
+        copies, keep = first[chunk]
         keep.wait()
         for copy in copies:
             copy.wait_recv()
 
-    for part in range(HALVES - 1):
-        arrive(part)
-        for pair in range(pairs):
-            filter_dft(pair, part, data_ref, rows_ref, table_ref, filt_ref, mid_ref)
-    arrive(HALVES - 1)
+    def sections(chunk):
+        rows_half = data_ref.shape[2]
+        for pos in range(2):
+            filter_chunk(
+                chunk, pos * rows_half // 2, rows_half // 2, data_ref, wide_ref, filt_ref
+            )
+            yield
+        for pos in range(2):
+            dft_chunk(chunk, pos * RADIX // 2, RADIX // 2, table_ref, filt_ref, mid_ref)
+            yield
+        radix_pass(chunk, mid_ref, send_ref)
+        yield
 
     turn_copies = {}
 
-    def send_turn(pair, turn):
+    def send_turn(chunk, turn):
         for rank in range(parts - 1):
-            turn_copy(pair, turn, far_first(me, parts, rank)).start()
-
-    for pair in range(pairs):
-        filter_dft(pair, HALVES - 1, data_ref, rows_ref, table_ref, filt_ref, mid_ref)
-        radix_pass(pair, mid_ref, send_ref)
-        for turn in range(rounds):
-            if pair * rounds + turn < WINDOW:
-                send_turn(pair, turn)
-            copies = [turn_copy(pair, turn, lax.rem(me + shift, parts)) for shift in range(1, parts)]
-            keep = pltpu.make_async_copy(
-                send_ref.at[pair, turn, me], recv_ref.at[pair, turn, me], keep_sem.at[pair, turn]
-            )
-            keep.start()
-            turn_copies[pair, turn] = (copies, keep)
-
-    def row_copy(kind, pair, turn, src, block, peer):
+            turn_copy(chunk, turn, far_first(me, parts, rank)).start()
+        copies = [turn_copy(chunk, turn, lax.rem(me + shift, parts)) for shift in range(1, parts)]
+        keep = pltpu.make_async_copy(
+            send_ref.at[chunk, turn, me], recv_ref.at[chunk, turn, me], keep_sem.at[chunk, turn]
+        )
+        keep.start()
+        turn_copies[chunk, turn] = (copies, keep)
+
+    def row_copy(kind, chunk, turn, src, block, peer):
         rows = pl.ds(turn * coarse_round, coarse_round)
         return pltpu.make_async_remote_copy(
             src_ref=src,
-            dst_ref=out_ref.at[block, rows, pair],
-            send_sem=row_send_sem.at[kind, pair, turn],
-            recv_sem=row_recv_sem.at[kind, pair, turn],
+            dst_ref=out_ref.at[block, rows, chunk],
+            send_sem=row_send_sem.at[kind, chunk, turn],
+            recv_sem=row_recv_sem.at[kind, chunk, turn],
             device_id={"bl": peer},
             device_id_type=mesh_id,
         )
 
-    order = [(pair, turn) for pair in range(pairs) for turn in range(rounds)]
+    order = [(chunk, turn) for chunk in range(CHUNKS) for turn in range(rounds)]
     across_copies, late = {}, []
 
-    def relay(pair, turn):
-        across_copies[pair, turn].wait_recv()
+    def relay(chunk, turn):
+        across_copies[chunk, turn].wait_recv()
         rows = pl.ds(turn * coarse_round, coarse_round)
-        copy = row_copy(2, pair, turn, out_ref.at[across, rows, pair], across, mate)
+        copy = row_copy(2, chunk, turn, out_ref.at[across, rows, chunk], across, mate)
         copy.start()
         late.append(copy)
 
-    lag = 3
-    for count, (pair, turn) in enumerate(order):
-        copies, keep = turn_copies[pair, turn]
+    def advance(count):
+        chunk, turn = order[count]
+        copies, keep = turn_copies[chunk, turn]
         keep.wait()
         for copy in copies:
             copy.wait_recv()
         if count + WINDOW < len(order):
             send_turn(*order[count + WINDOW])
-        merge_round(pair, turn, col, recv_ref, out_ref)
+        merge_round(chunk, turn, col, recv_ref, out_ref)
         rows = pl.ds(turn * coarse_round, coarse_round)
-        source = out_ref.at[col, rows, pair]
-        far = row_copy(0, pair, turn, source, col, across)
+        source = out_ref.at[col, rows, chunk]
+        far = row_copy(0, chunk, turn, source, col, across)
         far.start()
-        near = row_copy(1, pair, turn, source, col, mate)
+        near = row_copy(1, chunk, turn, source, col, mate)
         near.start()
-        across_copies[pair, turn] = far
+        across_copies[chunk, turn] = far
         late.append(near)
-        if count >= lag:
-            relay(*order[count - lag])
-    for position in order[len(order) - lag :]:
+        if count >= LAG:
+            relay(*order[count - LAG])
+
+    done = 0
+    for chunk in range(CHUNKS):
+        arrive(chunk)
+        for _ in sections(chunk):
+            if chunk > 0:
+                advance(done)
+                done += 1
+        if chunk == 0:
+            for position in order[:WINDOW]:
+                send_turn(*position)
+    for count in range(done, len(order)):
+        advance(count)
+    for position in order[len(order) - LAG :]:
         relay(*position)
     for copy in late:
         copy.wait()
@@ -525,37 +576,41 @@
 def exchange(voltages, coefs, table, parts, blocks):
     _, chan_count, rows_here = voltages.shape
     sub = chan_count // RADIX
-    pairs = parts // 2
     rows_round = AVG
     rounds = RADIX // parts * (sub // rows_round)
     coarse_here = chan_count // parts // AVG
-    depth = 4 * AVG
-    vmem = pl.BlockSpec(memory_space=pltpu.VMEM)
+    depth = SPECTRA * 2 * AVG
+    rows_half = chan_count // 2
+    lags = min(SPECTRA, coefs.shape[0])
     dma = pltpu.SemaphoreType.DMA
     return pl.pallas_call(
         functools.partial(exchange_kernel, parts),
-        in_specs=[vmem] * 3,
-        out_specs=vmem,
-        out_shape=pltpu.VMEM((blocks, coarse_here, pairs, rows_here, depth), jnp.bfloat16),
+        in_specs=[pl.BlockSpec(memory_space=pltpu.HBM)] * 3,
+        out_specs=pl.BlockSpec(memory_space=pltpu.VMEM),
+        out_shape=pltpu.VMEM((blocks + SPARE, coarse_here, CHUNKS, LANES, depth), jnp.bfloat16),
         scratch_shapes=[
-            pltpu.VMEM((HALVES, parts, chan_count // HALVES, LANES), jnp.bfloat16),
-            pltpu.VMEM((HALVES, parts, chan_count // HALVES, LANES), jnp.bfloat16),
-            pltpu.VMEM((HALVES, chan_count // HALVES, coefs.shape[0]), jnp.float32),
-            pltpu.VMEM((2, chan_count // HALVES, LANES), jnp.float32),
-            pltpu.VMEM((pairs, RADIX, 2 * sub, LANES), jnp.float32),
-            pltpu.VMEM((pairs, rounds, parts, 2, rows_round, LANES), jnp.bfloat16),
-            pltpu.VMEM((pairs, rounds, parts, 2, rows_round, LANES), jnp.bfloat16),
-            dma((HALVES, parts - 1)),
-            dma((HALVES, parts - 1)),
-            dma((pairs, rounds, parts - 1)),
-            dma((pairs, rounds, parts - 1)),
-            dma((pairs, rounds)),
-            dma((3, pairs, rounds)),
-            dma((3, pairs, rounds)),
-            dma((HALVES,)),
+            pltpu.VMEM(voltages.shape, voltages.dtype),
+            pltpu.VMEM(coefs.shape, coefs.dtype),
+            pltpu.VMEM(table.shape, table.dtype),
+            pltpu.VMEM((CHUNKS, parts, rows_half, LANES), jnp.bfloat16),
+            pltpu.VMEM((CHUNKS, parts, rows_half, LANES), jnp.bfloat16),
+            pltpu.VMEM((lags, rows_half, LANES), jnp.float32),
+            pltpu.VMEM((2, chan_count, LANES), jnp.float32),
+            pltpu.VMEM((CHUNKS, RADIX, 2 * sub, LANES), jnp.float32),
+            pltpu.VMEM((CHUNKS, rounds, parts, 2, rows_round, LANES), jnp.bfloat16),
+            pltpu.VMEM((CHUNKS, rounds, parts, 2, rows_round, LANES), jnp.bfloat16),
+            dma((CHUNKS + 2,)),
+            dma((CHUNKS, parts - 1)),
+            dma((CHUNKS, parts - 1)),
+            dma((CHUNKS, rounds, parts - 1)),
+            dma((CHUNKS, rounds, parts - 1)),
+            dma((CHUNKS, rounds)),
+            dma((3, CHUNKS, rounds)),
+            dma((3, CHUNKS, rounds)),
+            dma((CHUNKS,)),
         ],
         compiler_params=pltpu.CompilerParams(
-            collective_id=0, has_side_effects=True, vmem_limit_bytes=40 * 2**20
+            collective_id=0, has_side_effects=True, vmem_limit_bytes=44 * 2**20
         ),
         name="exchange",
     )(voltages, coefs, table)
@@ -588,32 +643,32 @@
 
 
 def tiles_kernel(norm_scale, ids_ref, owner_ref, data_ref, out_ref, slot_ref):
-    _, _, pairs, _, depth = data_ref.shape
+    depth = data_ref.shape[4]
     coarse = pl.program_id(0)
 
     @pl.when(coarse == 0)
     def _():
-        plan_slots(ids_ref, owner_ref, slot_ref, data_ref.shape[0])
-
-    half = depth // 2
+        plan_slots(ids_ref, owner_ref, slot_ref, ids_ref.shape[0])
+
     contract = (((1,), (1,)), ((), ()))
     for slot in range(out_ref.shape[2]):
         scale = jnp.where(slot_ref[2, slot] > 0, norm_scale, 0.0)
-        real, imag = None, None
-        for pair in range(pairs):
-            row = data_ref[slot_ref[0, slot], coarse, pair]
-            col = data_ref[slot_ref[1, slot], coarse, pair]
-            swapped = jnp.concatenate([row[:, half:], -row[:, :half]], axis=1)
-            first = lax.dot_general(row, col, contract, preferred_element_type=jnp.float32)
-            second = lax.dot_general(swapped, col, contract, preferred_element_type=jnp.float32)
-            real = first if real is None else real + first
-            imag = second if imag is None else imag + second
+        row = data_ref[slot_ref[0, slot], coarse].reshape(-1, depth)
+        col = data_ref[slot_ref[1, slot], coarse].reshape(-1, depth)
+        pieces = [row[:, pos : pos + AVG] for pos in range(0, depth, AVG)]
+        swapped = jnp.concatenate(
+            [-pieces[pos - 1] if pos % 2 else pieces[pos + 1] for pos in range(len(pieces))], axis=1
+        )
+        real = lax.dot_general(row, col, contract, preferred_element_type=jnp.float32)
+        imag = lax.dot_general(swapped, col, contract, preferred_element_type=jnp.float32)
         out_ref[0, 0, slot] = real * scale
         out_ref[1, 0, slot] = imag * scale
 
 
 def make_tiles(block_ids, tile_owner, gathered, norm_scale):
-    blocks, coarse_here, pairs, rows_here, depth = gathered.shape
+    _, coarse_here, chunks, lanes, _ = gathered.shape
+    blocks = block_ids.shape[0]
+    rows_here = chunks * lanes
     tile_count = blocks * (blocks + 1) // 2
     slot_cap = 2 * tile_count // blocks
     return pl.pallas_call(
@@ -628,7 +683,7 @@
             scratch_shapes=[pltpu.SMEM((3, slot_cap), jnp.int32)],
         ),
         out_shape=jax.ShapeDtypeStruct((2, coarse_here, slot_cap, rows_here, rows_here), jnp.float32),
-        compiler_params=pltpu.CompilerParams(vmem_limit_bytes=40 * 2**20),
+        compiler_params=pltpu.CompilerParams(vmem_limit_bytes=24 * 2**20),
         name="tiles",
     )(block_ids, tile_owner, gathered)
 
@@ -645,9 +700,8 @@
     parts = lax.axis_size("ft")
     fits = (
         voltages.shape[1] == chan_count
-        and parts % 2 == 0
-        and RADIX % parts == 0
-        and voltages.shape[2] == parts * LANES // 2
+        and parts == SPECTRA
+        and voltages.shape[2] == CHUNKS * LANES
         and chan_count == RADIX * LANES
         and (chan_count // RADIX) % AVG == 0
         and lax.axis_size("bl") == 4

time: 124 us -> 121 us (0.976)
  local copies, waits for them, and re-layouts: 4.03 us -> 0.01 us
    unnamed x10 -> x4, local copies, waits for them, and re-layouts: 4.03 us -> 0.01 us
where the time goes in v2:
time: 121 us
  Pallas kernels  121 us (100%)
    pallas_call x1, Pallas kernels, exchange(): pl.pallas_call(functools.partial(exchange_kernel, parts), in_specs=[pl.Bl...  110 us
    pallas_call x1, Pallas kernels, make_tiles(): pl.pallas_call(functools.partial(tiles_kernel, norm_scale), grid_spec=plt...  11.1 us

profile of v2, /device:TPU:1, one launch (start us, length us, event | category | flops | bytes accessed | tf_op | source)
XLA Modules:
  0.0 120.9 jit_solution(13682664173718938072)
XLA Ops:
  0.0 0.0 copy-start.1
  0.0 0.0 copy-start
  0.0 109.8 %exchange.1.data_ref = bf16[8,8,2,128,512]{4,3,2,1,0:T(8,128)(2,1)S(1)} custom-call(bf16[2,2048,256]{2,1,0:T(8,128)(2,1)} %volt_in.1, f32[8,2048]{1,0:T(8,128)} %coef_in.1, bf16[16,4,128,128]{3,2,1,0:T(8,128)(2,1)} %constant.2.clone.table_in), custom_call_target="tpu_custom_call" | custom-call | tf_op jit(solution)/shard_map/exchange/pallas_call | solution.py:586
  109.8 0.0 copy-done.1
  109.8 0.0 copy-done
  109.8 11.1 %tiles.1 = f32[2,8,5,256,256]{4,3,2,1,0:T(8,128)} custom-call(s32[4]{0:T(128)S(1)} %copy-done, s32[10]{0:T(128)S(1)} %copy-done.1, bf16[8,8,2,128,512]{4,3,2,1,0:T(8,128)(2,1)S(1)} %exchange.1.data_ref), custom_call_target="tpu_custom_call" | custom-call | tf_op jit(solution)/shard_map/tiles/pallas_call | solution.py:674
Async XLA Ops:
  0.0 109.8 %copy-start.1 = (s32[10]{0:T(128)S(1)}, s32[10]{0:T(128)}, u32[]{:S(2)}) copy-start(s32[10]{0:T(128)} %owner_ref.1) | copy-start | bytes 124
  0.0 109.8 %copy-start = (s32[4]{0:T(128)S(1)}, s32[4]{0:T(128)}, u32[]{:S(2)}) copy-start(s32[4]{0:T(128)} %ids_ref.1) | copy-start | bytes 52
